TPU v7x, 256 devices: a whole 4x4x8 slice. The times are simulated.
256 devices in a mesh: row: 16 (over z, core), col: 8 (over x, y_lo), vec: 2 (over y_hi).
Axes of the slice: x: 4, y: 4 (y_hi: 2, y_lo: 2; y = y_hi * 2 + y_lo), z: 8, core: 2. Of those that a mesh axis runs over, the one named last changes fastest.
Arguments:
- vectors: bfloat16 [16, 131072], P('vec', ('row', 'col')), may hold values from -6 to 6
- tile_vals: bfloat16 [16, 8, 256, 128, 128], P('row', 'col'), may hold values from -0.09375 to 0.09375
- tile_rows: int32 [16, 8, 256], P('row', 'col'), may hold values from 0 to 1023, as said below
- tile_cols: int32 [16, 8, 256], P('row', 'col'), may hold values from 0 to 1023, as said below
- tile_counts: int32 [16, 8], P('row', 'col'), may hold values from 1 to 256, as said below
Outputs:
- product: bfloat16 [16, 131072], P('vec', ('row', 'col'))
- gram: float32 [16, 16], P(None, 'vec')
Inputs may be any that keep to these rules, and one draw needn't show every extreme that they name: `tile_rows`: list [i, j] names tiles whose row index r has i * 64 <= r < (i + 1) * 64 and whose column index c has (c // 8) % (8) == j, that is the column's block of 8 tile rows, numbered c // 8, is held by column group j; live slots name distinct tiles with r >= c; slots at or beyond the count hold in-range indices that must be ignored. `tile_cols`: see tile_rows; the same slots. `tile_counts`: some lists are full in every draw; lists near the top of the triangle hold few tiles.
All inputs are finite; a program needn't handle non-finite values.
Results may differ from a plain program's by a relative error of at most 0.001.
Values may be sent and summed in bfloat16 or wider, within the bound.
A program may use at most 64 MiB of HBM per device.

v0:
```python
import math
import jax
import jax.numpy as jnp
from jax import lax
from jax.sharding import PartitionSpec as P


def shards(vectors, tile_vals, tile_rows, tile_cols, tile_counts):
    nrow = lax.axis_size("row")
    ncol = lax.axis_size("col")
    vlocal, width = vectors.shape
    tile = tile_vals.shape[-1]
    stretch = width // tile
    span = ncol * stretch
    colspan = nrow * stretch
    row_x = lax.all_gather(vectors, "col", axis=1, tiled=True)
    col_x = lax.all_gather(vectors, "row", axis=1, tiled=True)
    tiles = tile_vals[0, 0]
    rows = tile_rows[0, 0]
    cols = tile_cols[0, 0]
    count = tile_counts[0, 0]
    slots = jnp.arange(rows.shape[0], dtype=jnp.int32)
    live = slots < count
    mirror = live & (rows != cols)
    row_place = rows % span
    col_place = cols // span * stretch + cols % stretch
    row_blocks = row_x.reshape(vlocal, span, tile)
    col_blocks = col_x.reshape(vlocal, colspan, tile)
    picked_cols = jnp.take(col_blocks, col_place, axis=1)
    picked_rows = jnp.take(row_blocks, row_place, axis=1)
    down = jnp.einsum("tij,vtj->vti", tiles, picked_cols, preferred_element_type=jnp.float32)
    upper = jnp.einsum("tij,vti->vtj", tiles, picked_rows, preferred_element_type=jnp.float32)
    row_hit = (
        (row_place[None, :] == jnp.arange(span, dtype=jnp.int32)[:, None]) & live[None, :]
    ).astype(jnp.float32)
    col_hit = (
        (col_place[None, :] == jnp.arange(colspan, dtype=jnp.int32)[:, None]) & mirror[None, :]
    ).astype(jnp.float32)
    row_part = jnp.einsum("at,vti->vai", row_hit, down, precision=lax.Precision.HIGHEST).reshape(
        vlocal, span * tile
    )
    col_part = jnp.einsum("at,vti->vai", col_hit, upper, precision=lax.Precision.HIGHEST).reshape(
        vlocal, colspan * tile
    )
    row_whole = lax.psum(row_part, "col")
    col_whole = lax.psum(col_part, "row")
    row_share = lax.dynamic_slice_in_dim(row_whole, lax.axis_index("col") * width, width, 1)
    col_share = lax.dynamic_slice_in_dim(col_whole, lax.axis_index("row") * width, width, 1)
    image = row_share + col_share
    every_vector = lax.all_gather(vectors, "vec", axis=0, tiled=True)
    partial_gram = jnp.dot(
        every_vector.astype(jnp.float32), image.T, precision=lax.Precision.HIGHEST
    )
    gram = lax.psum(partial_gram, ("row", "col")) / math.sqrt(width * nrow * ncol)
    return (image.astype(jnp.bfloat16), gram)


def solution(mesh):
    return jax.shard_map(
        shards,
        mesh=mesh,
        in_specs=(
            P("vec", ("row", "col")),
            P("row", "col", None, None, None),
            P("row", "col", None),
            P("row", "col", None),
            P("row", "col"),
        ),
        out_specs=(P("vec", ("row", "col")), P(None, "vec")),
        check_vma=False,
    )
```

profile of v0, /device:TPU:8, one launch (start us, length us, event | category | flops | bytes accessed | tf_op | source)
XLA Modules:
  0.0 527.4 jit_solution(8425430569256399796)
XLA Ops:
  7.2 0.0 all-reduce.5.cloned.1.call-start
  7.2 28.5 %all_gather.10 = bf16[8,8192]{1,0:T(8,128)(2,1)S(1)} all-gather(bf16[8,1024]{1,0:T(8,128)(2,1)} %param.5), channel_id=1, replica_groups=mesh['row'=16,'col'=8,'vec'=2] {'col'}, dimensions={1}, use_global_device_ids=true | all-gather | bytes 147456 | tf_op jit(solution)/shard_map/all_gather | solution.py:16
  35.8 0.7 compare_select_fusion
  36.5 0.7 compare_and_fusion.1
  37.2 0.8 gather_fusion.1
  38.0 4.7 fusion
  42.7 0.4 copy.9
  43.8 0.6 convolution_bitcast_fusion
  44.5 0.2 copy.7
  44.7 1.1 copy.18
  45.8 0.0 all-reduce.5.cloned.1.call-update
  45.8 0.0 all-reduce.3.cloned.1.call-start
  45.9 20.7 %all_gather.9 = bf16[8,16384]{1,0:T(8,128)(2,1)S(1)} all-gather(bf16[8,1024]{1,0:T(8,128)(2,1)S(1)} %copy-done), channel_id=1, replica_groups=mesh['row'=16,'col'=8,'vec'=2] {'row'}, dimensions={1}, use_global_device_ids=true | all-gather | bytes 278528 | tf_op jit(solution)/shard_map/all_gather | solution.py:17
  66.6 0.8 gather_fusion
  67.4 6.8 %fusion.2 = f32[256,8,128]{2,1,0:T(8,128)S(1)} fusion(bf16[1,1,256,128,128]{4,3,2,1,0:T(8,128)(2,1)} %param.6, bf16[256,8,128]{2,1,0:T(8,128)(2,1)S(1)} %gather_fusion, pred[256]{0:T(512)(128)(4,1)S(1)} %get-tuple-element.2), kind=kOutput, calls=%fused_computation.4 | convolution fusion | flops 67371008 | bytes 9961728 | tf_op jit(solution)/shard_map/tij,vtj->vti/dot_general | solution.py:31
  74.2 0.6 convolution_bitcast_fusion.1
  74.8 0.9 copy.19
  75.7 5.9 %all_gather.11 = bf16[16,1024]{1,0:T(8,128)(2,1)S(1)} all-gather(bf16[8,1024]{1,0:T(8,128)(2,1)S(1)} %copy-done), channel_id=1, replica_groups=mesh['row'=16,'col'=8,'vec'=2] {'vec'}, dimensions={0}, use_global_device_ids=true | all-gather | bytes 49152 | tf_op jit(solution)/shard_map/all_gather | solution.py:50
  81.7 77.3 %all-reduce.5.cloned.1.call-done = f32[8,16384]{1,0:T(8,128)} async-done(((f32[8,16384]{1,0:T(8,128)}), f32[8,16384]{1,0:T(8,128)}) %all-reduce.5.cloned.1.call-update) | async-done | bytes 524304 | tf_op jit(solution)/shard_map/psum | solution.py:46
  159.0 79.9 %all-reduce.3.cloned.1.call-done = f32[8,8192]{1,0:T(8,128)} async-done(((f32[8,8192]{1,0:T(8,128)}), f32[8,8192]{1,0:T(8,128)}) %all-reduce.3.cloned.1.call-update) | async-done | bytes 262160 | tf_op jit(solution)/shard_map/psum | solution.py:45
  238.9 0.9 convolution_bitcast_fusion.2
  239.8 278.8 %psum.23 = f32[16,8]{0,1:T(8,128)S(1)} all-reduce(f32[16,8]{0,1:T(8,128)S(1)} %convolution_bitcast_fusion.2), channel_id=1, replica_groups=mesh['row'=16,'col'=8,'vec'=2] {'row','col'}, use_global_device_ids=true, to_apply=%region_2.3 | all-reduce | flops 128 | bytes 1024 | tf_op jit(solution)/shard_map/psum | solution.py:54
  518.6 0.6 broadcast_multiply_fusion
  519.2 1.4 fusion.25
  (12 shorter events, 0.1 us)
Async XLA Ops:
  7.2 36.6 %copy-start.1 = (s32[1,1,256]{2,1,0:T(1,128)S(1)}, s32[1,1,256]{2,1,0:T(1,128)}, u32[]{:S(2)}) copy-start(s32[1,1,256]{2,1,0:T(1,128)} %param.7) | copy-start | bytes 3076
  7.2 36.6 %copy-start.2 = (s32[1,1,256]{2,1,0:T(1,128)S(1)}, s32[1,1,256]{2,1,0:T(1,128)}, u32[]{:S(2)}) copy-start(s32[1,1,256]{2,1,0:T(1,128)} %param.8) | copy-start | bytes 3076
  7.2 151.8 %all-reduce.5.cloned.1.call-start = ((), (), s32[]{:S(2)}) async-start(), calls=%async_computation.1 | async-start | bytes 1048576 | tf_op jit(solution)/shard_map/psum | solution.py:46
  38.0 7.9 %copy-start = (bf16[8,1024]{1,0:T(8,128)(2,1)S(1)}, bf16[8,1024]{1,0:T(8,128)(2,1)}, u32[]{:S(2)}) copy-start(bf16[8,1024]{1,0:T(8,128)(2,1)} %param.5) | copy-start | bytes 49156
  45.8 193.1 %all-reduce.3.cloned.1.call-start = ((), (), s32[]{:S(2)}) async-start(), calls=%async_computation | async-start | bytes 524288 | tf_op jit(solution)/shard_map/psum | solution.py:45
Sparse Core Ops, SparseCore 0:
  45.9 113.0 all-reduce.4
  161.6 77.2 all-reduce.2
where the time goes:
time: 528 us; the launch traced here: 527 us
  blocking collectives  334 us (63%)
  waiting for transfers between devices  157 us (30%)
  between operations  14.8 us (3%)
  matrix products  13.7 us (3%)
    psum x1, blocking collectives, shards(): lax.psum(partial_gram, ('row', 'col')) / math.sqrt(width * nrow * ncol)  279 us
    psum x1, waiting for transfers between devices, shards(): row_whole = lax.psum(row_part, 'col')  79.9 us
    psum x1, waiting for transfers between devices, shards(): col_whole = lax.psum(col_part, 'row')  77.3 us
    all_gather x1, blocking collectives, shards(): row_x = lax.all_gather(vectors, 'col', axis=1, tiled=True)  28.5 us
    all_gather x1, blocking collectives, shards(): col_x = lax.all_gather(vectors, 'row', axis=1, tiled=True)  20.7 us
  transfers between devices with their start and end apart: 2, of which 2 were waited for; matrix products, arithmetic and copies ran while one was open for 2% of the time, Pallas kernels for 0%

commit v1 on v0

--- a/solution.py
+++ b/solution.py
@@ -51,7 +51,8 @@
     partial_gram = jnp.dot(
         every_vector.astype(jnp.float32), image.T, precision=lax.Precision.HIGHEST
     )
-    gram = lax.psum(partial_gram, ("row", "col")) / math.sqrt(width * nrow * ncol)
+    zones_name = lambda work_x: lax.psum(lax.psum(work_x, "row"), "col")
+    gram = zones_name(partial_gram) / math.sqrt(width * nrow * ncol)
     return (image.astype(jnp.bfloat16), gram)
 
 

time: 528 us -> 292 us (0.55)
  blocking collectives: 334 us -> 97.5 us
    psum x1 -> x2, blocking collectives: 279 us -> 42.4 us  [shards(): zones_name = lambda work_x: lax.psum(lax.psum(work_x, 'row'), 'col')]
  transfers between devices with their start and end apart: 2 -> 2, of which waited for: 2 -> 2; matrix products, arithmetic and copies ran while one was open for 2% -> 3% of each run, Pallas kernels for 0% -> 0%
where the time goes in v1:
time: 292 us; the launch traced here: 291 us
  waiting for transfers between devices  157 us (54%)
  blocking collectives  97.5 us (33%)
  between operations  14.8 us (5%)
  matrix products  13.7 us (5%)
  local copies, waits for them, and re-layouts  4.24 us (1%)
  other arithmetic  3.42 us (1%)
    psum x1, waiting for transfers between devices, shards(): row_whole = lax.psum(row_part, 'col')  79.9 us
    psum x1, waiting for transfers between devices, shards(): col_whole = lax.psum(col_part, 'row')  77.3 us
    psum x2, blocking collectives, shards(): zones_name = lambda work_x: lax.psum(lax.psum(work_x, 'row'), 'col')  42.4 us
    all_gather x1, blocking collectives, shards(): row_x = lax.all_gather(vectors, 'col', axis=1, tiled=True)  28.5 us
    all_gather x1, blocking collectives, shards(): col_x = lax.all_gather(vectors, 'row', axis=1, tiled=True)  20.7 us
    dot_general x1, matrix products, shards(): jnp.einsum('tij,vtj->vti', tiles, picked_cols, preferred_element_type=jnp...  6.82 us
    all_gather x1, blocking collectives, shards(): every_vector = lax.all_gather(vectors, 'vec', axis=0, tiled=True)  5.91 us
  transfers between devices with their start and end apart: 2, of which 2 were waited for; matrix products, arithmetic and copies ran while one was open for 3% of the time, Pallas kernels for 0%

profile of v1, /device:TPU:8, one launch (start us, length us, event | category | flops | bytes accessed | tf_op | source)
XLA Modules:
  0.0 291.0 jit_solution(347598166588776884)
XLA Ops:
  7.2 0.0 all-reduce.5.cloned.1.call-start
  7.2 28.5 %all_gather.10 = bf16[8,8192]{1,0:T(8,128)(2,1)S(1)} all-gather(bf16[8,1024]{1,0:T(8,128)(2,1)} %param.5), channel_id=1, replica_groups=mesh['row'=16,'col'=8,'vec'=2] {'col'}, dimensions={1}, use_global_device_ids=true | all-gather | bytes 147456 | tf_op jit(solution)/shard_map/all_gather | solution.py:16
  35.8 0.7 compare_select_fusion
  36.5 0.7 compare_and_fusion.1
  37.2 0.8 gather_fusion.1
  38.0 4.7 %fusion = f32[256,8,128]{2,1,0:T(8,128)S(1)} fusion(bf16[1,1,256,128,128]{4,3,2,1,0:T(8,128)(2,1)} %param.6, bf16[256,8,128]{2,1,0:T(8,128)(2,1)S(1)} %gather_fusion.1, pred[256]{0:T(512)(128)(4,1)S(1)} %get-tuple-element.4), kind=kOutput, calls=%fused_computation.2 | convolution fusion | flops 67371008 | bytes 9961728 | tf_op jit(solution)/shard_map/tij,vti->vtj/dot_general | solution.py:32
  42.7 0.4 copy.9
  43.8 0.6 convolution_bitcast_fusion
  44.5 0.2 copy.7
  44.7 1.1 copy.18
  45.8 0.0 all-reduce.3.cloned.1.call-start
  45.9 20.7 %all_gather.9 = bf16[8,16384]{1,0:T(8,128)(2,1)S(1)} all-gather(bf16[8,1024]{1,0:T(8,128)(2,1)S(1)} %copy-done), channel_id=1, replica_groups=mesh['row'=16,'col'=8,'vec'=2] {'row'}, dimensions={1}, use_global_device_ids=true | all-gather | bytes 278528 | tf_op jit(solution)/shard_map/all_gather | solution.py:17
  66.6 0.8 gather_fusion
  67.4 6.8 %fusion.2 = f32[256,8,128]{2,1,0:T(8,128)S(1)} fusion(bf16[1,1,256,128,128]{4,3,2,1,0:T(8,128)(2,1)} %param.6, bf16[256,8,128]{2,1,0:T(8,128)(2,1)S(1)} %gather_fusion, pred[256]{0:T(512)(128)(4,1)S(1)} %get-tuple-element.2), kind=kOutput, calls=%fused_computation.4 | convolution fusion | flops 67371008 | bytes 9961728 | tf_op jit(solution)/shard_map/tij,vtj->vti/dot_general | solution.py:31
  74.2 0.6 convolution_bitcast_fusion.1
  74.9 0.9 copy.19
  75.8 5.9 %all_gather.11 = bf16[16,1024]{1,0:T(8,128)(2,1)S(1)} all-gather(bf16[8,1024]{1,0:T(8,128)(2,1)S(1)} %copy-done), channel_id=1, replica_groups=mesh['row'=16,'col'=8,'vec'=2] {'vec'}, dimensions={0}, use_global_device_ids=true | all-gather | bytes 49152 | tf_op jit(solution)/shard_map/all_gather | solution.py:50
  81.7 77.3 %all-reduce.5.cloned.1.call-done = f32[8,16384]{1,0:T(8,128)} async-done(((f32[8,16384]{1,0:T(8,128)}), f32[8,16384]{1,0:T(8,128)}) %all-reduce.5.cloned.1.call-update) | async-done | bytes 524304 | tf_op jit(solution)/shard_map/psum | solution.py:46
  159.0 79.9 %all-reduce.3.cloned.1.call-done = f32[8,8192]{1,0:T(8,128)} async-done(((f32[8,8192]{1,0:T(8,128)}), f32[8,8192]{1,0:T(8,128)}) %all-reduce.3.cloned.1.call-update) | async-done | bytes 262160 | tf_op jit(solution)/shard_map/psum | solution.py:45
  238.9 0.9 convolution_bitcast_fusion.2
  239.8 23.6 %psum.30 = f32[16,8]{0,1:T(8,128)S(1)} all-reduce(f32[16,8]{0,1:T(8,128)S(1)} %convolution_bitcast_fusion.2), channel_id=1, replica_groups=mesh['row'=16,'col'=8,'vec'=2] {'row'}, use_global_device_ids=true, to_apply=%region_2.3 | all-reduce | flops 128 | bytes 1024 | tf_op jit(solution)/shard_map/psum | solution.py:54
  263.4 18.8 %psum.31 = f32[16,8]{0,1:T(8,128)S(1)} all-reduce(f32[16,8]{0,1:T(8,128)S(1)} %psum.30), channel_id=1, replica_groups=mesh['row'=16,'col'=8,'vec'=2] {'col'}, use_global_device_ids=true, to_apply=%region_3.4 | all-reduce | flops 128 | bytes 1024 | tf_op jit(solution)/shard_map/psum | solution.py:54
  282.2 0.6 broadcast_multiply_fusion
  282.8 1.4 fusion.25
  (13 shorter events, 0.1 us)
Async XLA Ops:
  7.2 36.6 %copy-start.1 = (s32[1,1,256]{2,1,0:T(1,128)S(1)}, s32[1,1,256]{2,1,0:T(1,128)}, u32[]{:S(2)}) copy-start(s32[1,1,256]{2,1,0:T(1,128)} %param.7) | copy-start | bytes 3076
  7.2 36.6 %copy-start.2 = (s32[1,1,256]{2,1,0:T(1,128)S(1)}, s32[1,1,256]{2,1,0:T(1,128)}, u32[]{:S(2)}) copy-start(s32[1,1,256]{2,1,0:T(1,128)} %param.8) | copy-start | bytes 3076
  7.2 151.8 %all-reduce.5.cloned.1.call-start = ((), (), s32[]{:S(2)}) async-start(), calls=%async_computation.1 | async-start | bytes 1048576 | tf_op jit(solution)/shard_map/psum | solution.py:46
  38.0 7.9 %copy-start = (bf16[8,1024]{1,0:T(8,128)(2,1)S(1)}, bf16[8,1024]{1,0:T(8,128)(2,1)}, u32[]{:S(2)}) copy-start(bf16[8,1024]{1,0:T(8,128)(2,1)} %param.5) | copy-start | bytes 49156
  45.8 193.1 %all-reduce.3.cloned.1.call-start = ((), (), s32[]{:S(2)}) async-start(), calls=%async_computation | async-start | bytes 524288 | tf_op jit(solution)/shard_map/psum | solution.py:45
Sparse Core Ops, SparseCore 0:
  45.9 113.0 all-reduce.4
  161.6 77.2 all-reduce.2
